TPU v7x, 32 devices: a whole 2x2x4 slice. The times are simulated.
32 devices in a mesh: area: 4 (over y, core), pos: 8 (over z, x).
Axes of the slice: x: 2, y: 2, z: 4, core: 2. Of those that a mesh axis runs over, the one named last changes fastest.
Arguments:
- exit_wave: bfloat16 [128, 2, 128, 128], P(('area', 'pos')), may hold values from -6 to 6
- amplitude: bfloat16 [128, 128, 128], P(('area', 'pos')), may hold values from 0.19921875 to 5
- probe: float32 [2, 128, 128], replicated, may hold values from -4 to 4
- offsets: int32 [128, 2], P(('area', 'pos')), may hold values from 0 to 127
- owner: int32 [128, 1], P(('area', 'pos')), may hold values from 0 to 7; in each aligned block of 4 rows (0 to 3, 4 to 7, ...) at most 2 rows name the same one
Outputs:
- new_wave: bfloat16 [128, 2, 128, 128], P(('area', 'pos'))
- object_field: float32 [2, 512, 1024], P(None, 'area', 'pos')
Inputs may be any that keep to these rules, and one draw needn't show every extreme that they name: owner names the object tile column that holds the position's patch centre; of the 4 positions of one device at most 2 name the same tile.
All inputs are finite; a program needn't handle non-finite values.
Results may differ from a plain program's by a relative error of at most 0.0059.
Values may be sent and summed in bfloat16 or wider, within the bound.
No kernel may reach another device: no remote copies, remote signals or barrier semaphores. Data moves between devices by JAX's collectives and lax.ppermute only.
A program may use at most 64 MiB of HBM per device.

v0:
```python
import math
import jax
import jax.numpy as jnp
from jax import lax
from jax.sharding import PartitionSpec as P

F = 128
TS = 128
C = 2


def passed_along(value, axis, steps):
    count = lax.axis_size(axis)
    first, last = (max(0, -steps), min(count, count - steps))
    return lax.ppermute(value, axis, [(source, source + steps) for source in range(first, last)])


def extended(cells, sides, width):
    for axis, dim in sides:
        count = lax.axis_size(axis)
        ends = count - 1
        head = lax.slice_in_dim(cells, 0, width, axis=dim)
        tail = lax.slice_in_dim(cells, cells.shape[dim] - width, cells.shape[dim], axis=dim)
        cells = jnp.concatenate(
            [
                lax.ppermute(tail, axis, [(i, (i + 1) % count) for i in range(ends)]),
                cells,
                lax.ppermute(head, axis, [((i + 1) % count, i) for i in range(ends)]),
            ],
            axis=dim,
        )
    return cells


def fold_rows(canvas):
    margin = F // 2
    summed = canvas
    for step in (1, -1):
        edge = canvas[:, TS + margin :, :] if step == 1 else canvas[:, :margin, :]
        arrived = passed_along(edge, "area", step)
        first = margin if step == 1 else TS
        summed = summed.at[:, first : first + margin, :].add(arrived)
    return summed[:, margin : margin + TS, :]


def fold_columns(canvas):
    margin = F // 2
    summed = canvas
    for step in (1, -1):
        edge = canvas[:, :, TS + margin :] if step == 1 else canvas[:, :, :margin]
        arrived = passed_along(edge, "pos", step)
        first = margin if step == 1 else TS
        summed = summed.at[:, :, first : first + margin].add(arrived)
    return summed[:, :, margin : margin + TS]


def left_multiply(mat_re, mat_im, data_re, data_im):
    highest = lax.Precision.HIGHEST
    out_re = jnp.einsum("kn,bnm->bkm", mat_re, data_re, precision=highest) - jnp.einsum(
        "kn,bnm->bkm", mat_im, data_im, precision=highest
    )
    out_im = jnp.einsum("kn,bnm->bkm", mat_re, data_im, precision=highest) + jnp.einsum(
        "kn,bnm->bkm", mat_im, data_re, precision=highest
    )
    return (out_re, out_im)


def right_multiply(data_re, data_im, mat_re, mat_im):
    highest = lax.Precision.HIGHEST
    out_re = jnp.einsum("bkm,ml->bkl", data_re, mat_re, precision=highest) - jnp.einsum(
        "bkm,ml->bkl", data_im, mat_im, precision=highest
    )
    out_im = jnp.einsum("bkm,ml->bkl", data_re, mat_im, precision=highest) + jnp.einsum(
        "bkm,ml->bkl", data_im, mat_re, precision=highest
    )
    return (out_re, out_im)


def cut_patches(source, row_starts, col_starts):
    return jax.vmap(lambda r, c: lax.dynamic_slice(source, (jnp.int32(0), r, c), (2, F, F)))(
        row_starts, col_starts
    )


def weighted_waves(waves_bf, probe_re, probe_im):
    waves_f = waves_bf.astype(jnp.float32)
    first = probe_re * waves_f[:, 0] + probe_im * waves_f[:, 1]
    second = probe_re * waves_f[:, 1] - probe_im * waves_f[:, 0]
    return jnp.stack([first, second], 1).astype(jnp.bfloat16)


def accumulate(contrib, meta, power_map):
    live = meta[:, 2]
    ordering = jnp.argsort(1 - live, stable=True)
    live_count = jnp.sum(live)

    def add_one(number, canvas):
        chosen = ordering[number]
        piece = jnp.concatenate([contrib[chosen].astype(jnp.float32), power_map[None]], 0)
        where = (jnp.int32(0), meta[chosen, 0], meta[chosen, 1])
        old = lax.dynamic_slice(canvas, where, (3, F, F))
        return lax.dynamic_update_slice(canvas, old + piece, where)

    canvas = lax.fori_loop(0, live_count, add_one, jnp.zeros((3, TS + F, TS + F), jnp.float32))
    summed = fold_columns(fold_rows(canvas))
    return (summed[0:2] / (summed[2] + 0.1)[None], ordering, live_count)


def relaxed_update(waves_bf, amps_bf, patch_bf, probe_re, probe_im):
    pixel = jnp.arange(F, dtype=jnp.int32)
    product = pixel[:, None] * pixel[None, :] % F
    angle = product.astype(jnp.float32) * (2.0 * math.pi / F)
    scale_by = 1.0 / math.sqrt(F)
    twiddle_re = jnp.cos(angle) * scale_by
    twiddle_im = -jnp.sin(angle) * scale_by
    waves_f = waves_bf.astype(jnp.float32)
    patch_f = patch_bf.astype(jnp.float32)
    proj_re = probe_re * patch_f[:, 0] - probe_im * patch_f[:, 1]
    proj_im = probe_re * patch_f[:, 1] + probe_im * patch_f[:, 0]
    trial_re = 2.0 * proj_re - waves_f[:, 0]
    trial_im = 2.0 * proj_im - waves_f[:, 1]
    half_re, half_im = left_multiply(twiddle_re, twiddle_im, trial_re, trial_im)
    spectrum_re, spectrum_im = right_multiply(half_re, half_im, twiddle_re, twiddle_im)
    modulus = jnp.sqrt(spectrum_re * spectrum_re + spectrum_im * spectrum_im + 0.01)
    ratio = amps_bf.astype(jnp.float32) / modulus
    fitted_re = spectrum_re * ratio
    fitted_im = spectrum_im * ratio
    half_re, half_im = left_multiply(twiddle_re, -twiddle_im, fitted_re, fitted_im)
    back_re, back_im = right_multiply(half_re, half_im, twiddle_re, -twiddle_im)
    new_re = 0.75 * waves_f[:, 0] - 0.5 * proj_re + 0.75 * back_re
    new_im = 0.75 * waves_f[:, 1] - 0.5 * proj_im + 0.75 * back_im
    return jnp.stack([new_re, new_im], 1).astype(jnp.bfloat16)


def body(exit_wave, amplitude, probe, offsets, owner):
    margin = F // 2
    columns_count = lax.axis_size("pos")
    probe_re = probe[0]
    probe_im = probe[1]
    power_map = probe_re * probe_re + probe_im * probe_im
    target = owner[:, 0]
    one_hot = (target[:, None] == jnp.arange(columns_count, dtype=jnp.int32)[None, :]).astype(
        jnp.int32
    )
    rank_in = jnp.sum((jnp.cumsum(one_hot, axis=0) - 1) * one_hot, axis=1)
    slot_flat = target * C + rank_in
    slot_total = columns_count * C
    described = jnp.concatenate([offsets, jnp.ones((offsets.shape[0], 1), jnp.int32)], 1)
    send_meta = jnp.zeros((slot_total, 3), jnp.int32).at[slot_flat].set(described)
    contrib = weighted_waves(exit_wave, probe_re, probe_im)
    send_wave = jnp.zeros((slot_total, 2, F, F), jnp.bfloat16).at[slot_flat].set(contrib)
    got_wave, got_meta = (
        lax.all_to_all(send_wave, "pos", split_axis=0, concat_axis=0, tiled=True),
        lax.all_to_all(send_meta, "pos", split_axis=0, concat_axis=0, tiled=True),
    )
    object_tile, ordering, live_count = accumulate(got_wave, got_meta, power_map)
    object_half = object_tile.astype(jnp.bfloat16)
    strip = extended(object_half, (("area", 1),), margin)
    band_rows = lax.all_gather(strip, "pos", axis=2, tiled=True)
    band_rows = jnp.pad(band_rows, ((0, 0), (0, 0), (margin, margin)))
    own_patch = cut_patches(band_rows, offsets[:, 0], target * TS + offsets[:, 1])
    new_wave = relaxed_update(exit_wave, amplitude, own_patch, probe_re, probe_im)
    return (new_wave, object_tile)


def solution(mesh):
    return jax.shard_map(
        body,
        mesh=mesh,
        in_specs=(
            P(("area", "pos"), None, None, None),
            P(("area", "pos"), None, None),
            P(),
            P(("area", "pos"), None),
            P(("area", "pos"), None),
        ),
        out_specs=(P(("area", "pos"), None, None, None), P(None, "area", "pos")),
        check_vma=False,
    )
```

profile of v0, /device:TPU:0, one launch (start us, length us, event | category | flops | bytes accessed | tf_op | source)
XLA Modules:
  0.0 265.7 jit_solution(17552448648142886674)
XLA Ops:
  7.9 0.8 select_reduce_fusion
  8.8 0.8 copy.121
  9.5 0.8 compare_select_fusion.1
  10.3 1.2 scatter_custom_fusion
  11.5 7.3 %all-to-all-start = ((s32[8,2,3]{2,1,0:T(2,128)}), s32[8,2,3]{2,1,0:T(2,128)S(1)}, u32[]{:S(2)}, u32[]{:S(2)}) async-start(s32[8,2,3]{2,1,0:T(2,128)} %bitcast.10), calls=%async_computation | async-start | bytes 16384 | tf_op jit(solution)/shard_map/all_to_all | solution.py:154
  18.7 1.0 copy_convert_fusion
  19.7 0.9 slice_bitcast_fusion.3
  20.8 1.2 broadcast_in_dim.11
  22.0 2.2 scatter_fusion
  24.2 1.1 all-to-all-done
  25.3 5.0 %all-to-all-start.1 = ((bf16[16,2,128,128]{3,2,1,0:T(8,128)(2,1)}), bf16[16,2,128,128]{3,2,1,0:T(8,128)(2,1)S(1)}, u32[]{:S(2)}, u32[]{:S(2)}) async-start(bf16[16,2,128,128]{3,2,1,0:T(8,128)(2,1)} %scatter_fusion), calls=%async_computation.1 | async-start | bytes 2097152 | tf_op jit(solution)/shard_map/all_to_all | solution.py:153
  31.1 1.3 sort.17
  32.3 23.4 %all-to-all-done.1 = bf16[16,2,128,128]{3,2,1,0:T(8,128)(2,1)S(1)} async-done(((bf16[16,2,128,128]{3,2,1,0:T(8,128)(2,1)}), bf16[16,2,128,128]{3,2,1,0:T(8,128)(2,1)S(1)}, u32[]{:S(2)}, u32[]{:S(2)}) %all-to-all-start.1) | async-done | bytes 1048608 | tf_op jit(solution)/shard_map/all_to_all | solution.py:153
  55.8 62.8 %while.15 = (s32[]{:T(128)}, f32[3,256,256]{2,1,0:T(8,128)S(1)}, s32[]{:T(128)}, s32[16]{0:T(128)S(1)}, s32[16,3]{0,1:T(4,128)S(1)}, /*index=5*/bf16[16,2,128,12...) while((s32[]{:T(128)}, f32[3,256,256]{2,1,0:T(8,128)S(1)}, ...), condition=%wide.region_7.8_spmd, body=%wide.region_6.7_spmd.sunk | while | flops 131086 | bytes 1179941 | solution.py:104
  63.3 2.8 %dynamic_update_slice.4 = f32[3,256,256]{2,1,0:T(8,128)S(1)} dynamic-update-slice(f32[3,256,256]{2,1,0:T(8,128)S(1)} %get-tuple-element.257, f32[3,128,128]{2,1,0:T(8,128)S(1)} %maximum_add_fusion.2, s32[]{:T(128)} %constant.154.clone.1..sunk, s32[]{:T(128)S(6)} %select_n.138, s32[]{:T(128)S(6)} %select_n.139) | dynamic-update-slice | bytes 393220 | tf_op jit(solution)/shard_map/while/body/dynamic_update_slice | solution.py:102
  73.5 2.9 %dynamic_update_slice.4 = f32[3,256,256]{2,1,0:T(8,128)S(1)} dynamic-update-slice(f32[3,256,256]{2,1,0:T(8,128)S(1)} %get-tuple-element.257, f32[3,128,128]{2,1,0:T(8,128)S(1)} %maximum_add_fusion.2, s32[]{:T(128)} %constant.154.clone.1..sunk, s32[]{:T(128)S(6)} %select_n.138, s32[]{:T(128)S(6)} %select_n.139) | dynamic-update-slice | bytes 393220 | tf_op jit(solution)/shard_map/while/body/dynamic_update_slice | solution.py:102
  83.9 2.9 %dynamic_update_slice.4 = f32[3,256,256]{2,1,0:T(8,128)S(1)} dynamic-update-slice(f32[3,256,256]{2,1,0:T(8,128)S(1)} %get-tuple-element.257, f32[3,128,128]{2,1,0:T(8,128)S(1)} %maximum_add_fusion.2, s32[]{:T(128)} %constant.154.clone.1..sunk, s32[]{:T(128)S(6)} %select_n.138, s32[]{:T(128)S(6)} %select_n.139) | dynamic-update-slice | bytes 393220 | tf_op jit(solution)/shard_map/while/body/dynamic_update_slice | solution.py:102
  94.3 2.8 %dynamic_update_slice.4 = f32[3,256,256]{2,1,0:T(8,128)S(1)} dynamic-update-slice(f32[3,256,256]{2,1,0:T(8,128)S(1)} %get-tuple-element.257, f32[3,128,128]{2,1,0:T(8,128)S(1)} %maximum_add_fusion.2, s32[]{:T(128)} %constant.154.clone.1..sunk, s32[]{:T(128)S(6)} %select_n.138, s32[]{:T(128)S(6)} %select_n.139) | dynamic-update-slice | bytes 393220 | tf_op jit(solution)/shard_map/while/body/dynamic_update_slice | solution.py:102
  104.5 3.0 %dynamic_update_slice.4 = f32[3,256,256]{2,1,0:T(8,128)S(1)} dynamic-update-slice(f32[3,256,256]{2,1,0:T(8,128)S(1)} %get-tuple-element.257, f32[3,128,128]{2,1,0:T(8,128)S(1)} %maximum_add_fusion.2, s32[]{:T(128)} %constant.154.clone.1..sunk, s32[]{:T(128)S(6)} %select_n.138, s32[]{:T(128)S(6)} %select_n.139) | dynamic-update-slice | bytes 393220 | tf_op jit(solution)/shard_map/while/body/dynamic_update_slice | solution.py:102
  115.0 2.9 %dynamic_update_slice.4 = f32[3,256,256]{2,1,0:T(8,128)S(1)} dynamic-update-slice(f32[3,256,256]{2,1,0:T(8,128)S(1)} %get-tuple-element.257, f32[3,128,128]{2,1,0:T(8,128)S(1)} %maximum_add_fusion.2, s32[]{:T(128)} %constant.154.clone.1..sunk, s32[]{:T(128)S(6)} %select_n.138, s32[]{:T(128)S(6)} %select_n.139) | dynamic-update-slice | bytes 393220 | tf_op jit(solution)/shard_map/while/body/dynamic_update_slice | solution.py:102
  118.6 1.3 collective-permute-start
  119.9 1.0 collective-permute-done
  121.0 1.3 collective-permute-start.1
  122.3 2.0 collective-permute-done.1
  124.5 1.3 collective-permute-start.2
  125.9 1.3 collective-permute-start.3
  127.2 1.8 collective-permute-done.2
  129.1 1.3 scatter-add.16
  130.5 54.6 %collective-permute-done.3 = f32[3,128,64]{2,1,0:T(8,128)S(1)} collective-permute-done((f32[3,128,64]{2,1,0:T(8,128)S(1)}, f32[3,128,64]{2,1,0:T(8,128)S(1)}, u32[]{:S(2)}, u32[]{:S(2)}) %collective-permute-start.3) | collective-permute-done | bytes 98336 | tf_op jit(solution)/shard_map/ppermute | solution.py:15
  185.6 0.8 fusion.145
  186.4 4.8 %collective-permute-start.4 = (bf16[2,64,128]{2,1,0:T(8,128)(2,1)S(1)}, bf16[2,64,128]{2,1,0:T(8,128)(2,1)S(1)}, u32[]{:S(2)}, u32[]{:S(2)}) collective-permute-start(bf16[2,64,128]{2,1,0:T(8,128)(2,1)S(1)} %get-tuple-element.161), channel_id=1, source_target_pairs={{0,8},{8,16},{16,24},{1,9},{9,17},{17,25},{2,10},{10,18},{18,26},{... | collective-permute-start | bytes 98312 | tf_op jit(solution)/shard_map/ppermute | solution.py:26
  191.2 1.3 collective-permute-start.5
  192.5 2.3 collective-permute-done.5
  195.6 40.4 %all-gather.2.cloned.1.call-done = bf16[2,256,1024]{2,1,0:T(8,128)(2,1)} async-done(((bf16[2,256,128]{2,1,0:T(8,128)(2,1)}), bf16[2,256,1024]{2,1,0:T(8,128)(2,1)}) %all-gather.2.cloned.1.call-update) | async-done | bytes 1048592 | tf_op jit(solution)/shard_map/all_gather | solution.py:159
  236.0 1.9 pad.13
  237.9 8.0 %while.16 = (s32[]{:T(128)}, bf16[2,256,1152]{2,1,0:T(8,128)(2,1)S(1)}, s32[4,3]{1,0:T(4,128)S(1)}, bf16[4,2,128,128]{3,2,0,1:T(8,128)(2,1)S(1)}, s32[]{:T(128)}) while((s32[]{:T(128)}, bf16[2,256,1152]{2,1,0:T(8,128)(2,1)S(1)}, s32[4,3]{1,0:T(4,128)S(1)}, bf16[4,2,128,128]{3,2,0,1:T(8,128)(2,1)S(1)}, s32[]{:T(128)}) %tuple.76), condition=%wide.while_cond.4, body=%wide.while_body.4.sunk | while | flops 2 | bytes 131189 | solution.py:80
  238.5 1.3 bitcast_dynamic-update-slice_fusion.2
  240.5 1.3 bitcast_dynamic-update-slice_fusion.2
  242.4 1.3 bitcast_dynamic-update-slice_fusion.2
  244.3 1.3 bitcast_dynamic-update-slice_fusion.2
  246.0 0.7 fusion.18
  246.8 0.8 fusion.17
  247.5 0.8 fusion.7
  249.7 0.7 fusion.6
  252.0 0.8 fusion.34
  252.8 0.8 fusion.38
  253.6 0.8 fusion.5
  255.8 0.8 fusion.4
  (76 shorter events, 20.9 us)
Async XLA Ops:
  11.5 13.8 %all-to-all-start = ((s32[8,2,3]{2,1,0:T(2,128)}), s32[8,2,3]{2,1,0:T(2,128)S(1)}, u32[]{:S(2)}, u32[]{:S(2)}) async-start(s32[8,2,3]{2,1,0:T(2,128)} %bitcast.10), calls=%async_computation | async-start | bytes 16384 | tf_op jit(solution)/shard_map/all_to_all | solution.py:154
  24.2 6.2 %copy-start.1 = (f32[2,128,128]{2,1,0:T(8,128)S(1)}, f32[2,128,128]{2,1,0:T(8,128)}, u32[]{:S(2)}) copy-start(f32[2,128,128]{2,1,0:T(8,128)} %param.17) | copy-start | bytes 393220
  25.3 30.5 %all-to-all-start.1 = ((bf16[16,2,128,128]{3,2,1,0:T(8,128)(2,1)}), bf16[16,2,128,128]{3,2,1,0:T(8,128)(2,1)S(1)}, u32[]{:S(2)}, u32[]{:S(2)}) async-start(bf16[16,2,128,128]{3,2,1,0:T(8,128)(2,1)} %scatter_fusion), calls=%async_computation.1 | async-start | bytes 2097152 | tf_op jit(solution)/shard_map/all_to_all | solution.py:153
  30.3 205.7 %all-gather.2.cloned.1.call-start = ((), (), s32[]{:S(2)}) async-start(), calls=%async_computation.2 | async-start | bytes 1179648 | tf_op jit(solution)/shard_map/all_gather | solution.py:159
  118.6 2.4 collective-permute-start
  121.0 3.3 %collective-permute-start.1 = (f32[3,64,256]{2,1,0:T(8,128)S(1)}, f32[3,64,256]{2,1,0:T(8,128)S(1)}, u32[]{:S(2)}, u32[]{:S(2)}) collective-permute-start(f32[3,64,256]{2,1,0:T(8,128)S(1)} %get-tuple-element.153), channel_id=1, source_target_pairs={{8,0},{16,8},{24,16},{9,1},{17,9},{25,17},{10,2},{18,10},{26,18},{... | collective-permute-start | bytes 589832 | tf_op jit(solution)/shard_map/ppermute | solution.py:15
  124.5 4.5 %collective-permute-start.2 = (f32[3,128,64]{2,1,0:T(8,128)S(1)}, f32[3,128,64]{2,1,0:T(8,128)S(1)}, u32[]{:S(2)}, u32[]{:S(2)}) collective-permute-start(f32[3,128,64]{2,1,0:T(8,128)S(1)} %get-tuple-element.152), channel_id=1, source_target_pairs={{0,1},{1,2},{2,3},{3,4},{4,5},{5,6},{6,7},{8,9},{9,10},{10,11},{11... | collective-permute-start | bytes 294920 | tf_op jit(solution)/shard_map/ppermute | solution.py:15
  125.9 59.2 %collective-permute-start.3 = (f32[3,128,64]{2,1,0:T(8,128)S(1)}, f32[3,128,64]{2,1,0:T(8,128)S(1)}, u32[]{:S(2)}, u32[]{:S(2)}) collective-permute-start(f32[3,128,64]{2,1,0:T(8,128)S(1)} %get-tuple-element.151), channel_id=1, source_target_pairs={{1,0},{2,1},{3,2},{4,3},{5,4},{6,5},{7,6},{9,8},{10,9},{11,10},{12... | collective-permute-start | bytes 294920 | tf_op jit(solution)/shard_map/ppermute | solution.py:15
  186.4 6.1 %collective-permute-start.4 = (bf16[2,64,128]{2,1,0:T(8,128)(2,1)S(1)}, bf16[2,64,128]{2,1,0:T(8,128)(2,1)S(1)}, u32[]{:S(2)}, u32[]{:S(2)}) collective-permute-start(bf16[2,64,128]{2,1,0:T(8,128)(2,1)S(1)} %get-tuple-element.161), channel_id=1, source_target_pairs={{0,8},{8,16},{16,24},{1,9},{9,17},{17,25},{2,10},{10,18},{18,26},{... | collective-permute-start | bytes 98312 | tf_op jit(solution)/shard_map/ppermute | solution.py:26
  191.2 3.6 %collective-permute-start.5 = (bf16[2,64,128]{2,1,0:T(8,128)(2,1)S(1)}, bf16[2,64,128]{2,1,0:T(8,128)(2,1)S(1)}, u32[]{:S(2)}, u32[]{:S(2)}) collective-permute-start(bf16[2,64,128]{2,1,0:T(8,128)(2,1)S(1)} %get-tuple-element.162), channel_id=1, source_target_pairs={{8,0},{16,8},{24,16},{9,1},{17,9},{25,17},{10,2},{18,10},{26,18},{... | collective-permute-start | bytes 98312 | tf_op jit(solution)/shard_map/ppermute | solution.py:28
  249.7 2.2 copy-start
Sparse Core Ops, SparseCore 0:
  195.6 40.3 all-gather.1
where the time goes:
time: 267 us; the launch traced here: 266 us
  waiting for transfers between devices  127 us (48%)
  local copies, waits for them, and re-layouts  43.4 us (16%)
  loops' own time  37.5 us (14%)
  starting transfers between devices  23.6 us (9%)
  between operations  14.4 us (5%)
  matrix products  12 us (4%)
  other arithmetic  8.18 us (3%)
    ppermute x4, waiting for transfers between devices, passed_along(): lax.ppermute(value, axis, [(source, source + steps) for source in range(f...  59.5 us
    all_gather x1, waiting for transfers between devices, body(): band_rows = lax.all_gather(strip, 'pos', axis=2, tiled=True)  40.4 us
    another operation x1, loops' own time, accumulate(): lax.fori_loop(0, live_count, add_one, jnp.zeros((3, TS + F, TS + F), jnp....  37.2 us
    all_to_all x1, waiting for transfers between devices, body(): lax.all_to_all(send_wave, 'pos', split_axis=0, concat_axis=0, tiled=True)  23.4 us
    dynamic_update_slice x6, local copies, waits for them, and re-layouts, add_one(): return lax.dynamic_update_slice(canvas, old + piece, where)  17.2 us
    gather x12, local copies, waits for them, and re-layouts  7.71 us
    all_to_all x1, starting transfers between devices, body(): lax.all_to_all(send_meta, 'pos', split_axis=0, concat_axis=0, tiled=True)  7.28 us
  transfers between devices with their start and end apart: 9, of which 8 were waited for; matrix products, arithmetic and copies ran while one was open for 3% of the time, Pallas kernels for 0%

commit v1 on v0

--- a/solution.py
+++ b/solution.py
@@ -1,3 +1,4 @@
+import functools
 import math
 import jax
 import jax.numpy as jnp
@@ -7,6 +8,23 @@
 F = 128
 TS = 128
 C = 2
+
+
+def view_run(block_here, axis_key, pos_dim):
+    many = lax.axis_size(axis_key)
+    return lax.all_to_all(
+        jnp.tile(
+            block_here,
+            list(map(lambda to_i: many if to_i == pos_dim else 1, range(block_here.ndim))),
+        ),
+        axis_name=axis_key,
+        split_axis=pos_dim,
+        concat_axis=pos_dim,
+        tiled=True,
+    )
+
+
+track_files_here = functools.partial(view_run, axis_key="pos", pos_dim=2)
 
 
 def passed_along(value, axis, steps):
@@ -156,7 +174,7 @@
     object_tile, ordering, live_count = accumulate(got_wave, got_meta, power_map)
     object_half = object_tile.astype(jnp.bfloat16)
     strip = extended(object_half, (("area", 1),), margin)
-    band_rows = lax.all_gather(strip, "pos", axis=2, tiled=True)
+    band_rows = track_files_here(strip)
     band_rows = jnp.pad(band_rows, ((0, 0), (0, 0), (margin, margin)))
     own_patch = cut_patches(band_rows, offsets[:, 0], target * TS + offsets[:, 1])
     new_wave = relaxed_update(exit_wave, amplitude, own_patch, probe_re, probe_im)

time: 267 us -> 252 us (0.944)
  between operations: 14.4 us -> 1 us
  waiting for transfers between devices: 127 us -> 115 us
  starting transfers between devices: 23.6 us -> 27.8 us
  local copies, waits for them, and re-layouts: 43.4 us -> 46.4 us
    all_gather x1 -> x0, waiting for transfers between devices: 40.4 us -> none  [body(): band_rows = lax.all_gather(strip, 'pos', axis=2, tiled=True)]
    all_to_all x0 -> x1, waiting for transfers between devices: none -> 26.4 us  [view_run(): lax.all_to_all(jnp.tile(block_here, list(map(lambda to_i: many if to_i ==...]
    all_to_all x0 -> x1, starting transfers between devices: none -> 4.19 us  [view_run(): lax.all_to_all(jnp.tile(block_here, list(map(lambda to_i: many if to_i ==...]
    gather x12 -> x20, local copies, waits for them, and re-layouts: 7.71 us -> 8.8 us
  transfers between devices with their start and end apart: 9 -> 9, of which waited for: 8 -> 8; matrix products, arithmetic and copies ran while one was open for 3% -> 4% of each run, Pallas kernels for 0% -> 0%
where the time goes in v1:
time: 252 us; the launch traced here: 250 us
  waiting for transfers between devices  115 us (46%)
  local copies, waits for them, and re-layouts  46.4 us (18%)
  loops' own time  40 us (16%)
  starting transfers between devices  27.8 us (11%)
  matrix products  12 us (5%)
  other arithmetic  7.59 us (3%)
    ppermute x4, waiting for transfers between devices, passed_along(): lax.ppermute(value, axis, [(source, source + steps) for source in range(f...  62 us
    another operation x1, loops' own time, accumulate(): lax.fori_loop(0, live_count, add_one, jnp.zeros((3, TS + F, TS + F), jnp....  39.7 us
    all_to_all x1, waiting for transfers between devices, view_run(): lax.all_to_all(jnp.tile(block_here, list(map(lambda to_i: many if to_i ==...  26.4 us
    all_to_all x1, waiting for transfers between devices, body(): lax.all_to_all(send_wave, 'pos', split_axis=0, concat_axis=0, tiled=True)  23.3 us
    dynamic_update_slice x6, local copies, waits for them, and re-layouts, add_one(): return lax.dynamic_update_slice(canvas, old + piece, where)  17.2 us
    gather x20, local copies, waits for them, and re-layouts  8.8 us
    all_to_all x1, starting transfers between devices, body(): lax.all_to_all(send_meta, 'pos', split_axis=0, concat_axis=0, tiled=True)  7.28 us
    ppermute x4, starting transfers between devices, passed_along(): lax.ppermute(value, axis, [(source, source + steps) for source in range(f...  5.19 us
  transfers between devices with their start and end apart: 9, of which 8 were waited for; matrix products, arithmetic and copies ran while one was open for 4% of the time, Pallas kernels for 0%

profile of v1, /device:TPU:0, one launch (start us, length us, event | category | flops | bytes accessed | tf_op | source)
XLA Modules:
  0.0 249.8 jit_solution(2084400669919838624)
XLA Ops:
  1.4 0.8 select_reduce_fusion
  2.2 0.8 copy.126
  3.0 0.8 compare_select_fusion.1
  3.8 1.2 scatter_custom_fusion
  4.9 7.3 %all-to-all-start = ((s32[8,2,3]{2,1,0:T(2,128)}), s32[8,2,3]{2,1,0:T(2,128)S(1)}, u32[]{:S(2)}, u32[]{:S(2)}) async-start(s32[8,2,3]{2,1,0:T(2,128)} %bitcast.10), calls=%async_computation | async-start | bytes 16384 | tf_op jit(solution)/shard_map/all_to_all | solution.py:172
  12.2 1.0 copy_convert_fusion
  13.2 0.9 slice_bitcast_fusion.3
  14.2 1.2 broadcast_in_dim.11
  15.4 2.2 scatter_fusion
  17.7 1.1 all-to-all-done
  18.7 5.0 %all-to-all-start.1 = ((bf16[16,2,128,128]{3,2,1,0:T(8,128)(2,1)}), bf16[16,2,128,128]{3,2,1,0:T(8,128)(2,1)S(1)}, u32[]{:S(2)}, u32[]{:S(2)}) async-start(bf16[16,2,128,128]{3,2,1,0:T(8,128)(2,1)} %scatter_fusion), calls=%async_computation.1 | async-start | bytes 2097152 | tf_op jit(solution)/shard_map/all_to_all | solution.py:171
  24.5 1.3 sort.17
  25.8 23.3 %all-to-all-done.1 = bf16[16,2,128,128]{3,2,1,0:T(8,128)(2,1)S(1)} async-done(((bf16[16,2,128,128]{3,2,1,0:T(8,128)(2,1)}), bf16[16,2,128,128]{3,2,1,0:T(8,128)(2,1)S(1)}, u32[]{:S(2)}, u32[]{:S(2)}) %all-to-all-start.1) | async-done | bytes 1048608 | tf_op jit(solution)/shard_map/all_to_all | solution.py:171
  49.3 65.8 %while.15 = (s32[]{:T(128)}, f32[3,256,256]{2,1,0:T(8,128)S(1)}, s32[]{:T(128)}, s32[16]{0:T(128)S(1)}, s32[16,3]{0,1:T(4,128)S(1)}, /*index=5*/bf16[16,2,128,12...) while((s32[]{:T(128)}, f32[3,256,256]{2,1,0:T(8,128)S(1)}, ...), condition=%wide.region_7.8_spmd, body=%wide.region_6.7_spmd.sunk | while | flops 131086 | bytes 1179941 | solution.py:122
  57.2 2.8 %dynamic_update_slice.4 = f32[3,256,256]{2,1,0:T(8,128)S(1)} dynamic-update-slice(f32[3,256,256]{2,1,0:T(8,128)S(1)} %get-tuple-element.257, f32[3,128,128]{2,1,0:T(8,128)S(1)} %maximum_add_fusion.2, s32[]{:T(128)} %constant.154.clone.1..sunk, s32[]{:T(128)S(6)} %select_n.138, s32[]{:T(128)S(6)} %select_n.139) | dynamic-update-slice | bytes 393220 | tf_op jit(solution)/shard_map/while/body/dynamic_update_slice | solution.py:120
  68.0 2.9 %dynamic_update_slice.4 = f32[3,256,256]{2,1,0:T(8,128)S(1)} dynamic-update-slice(f32[3,256,256]{2,1,0:T(8,128)S(1)} %get-tuple-element.257, f32[3,128,128]{2,1,0:T(8,128)S(1)} %maximum_add_fusion.2, s32[]{:T(128)} %constant.154.clone.1..sunk, s32[]{:T(128)S(6)} %select_n.138, s32[]{:T(128)S(6)} %select_n.139) | dynamic-update-slice | bytes 393220 | tf_op jit(solution)/shard_map/while/body/dynamic_update_slice | solution.py:120
  78.9 2.9 %dynamic_update_slice.4 = f32[3,256,256]{2,1,0:T(8,128)S(1)} dynamic-update-slice(f32[3,256,256]{2,1,0:T(8,128)S(1)} %get-tuple-element.257, f32[3,128,128]{2,1,0:T(8,128)S(1)} %maximum_add_fusion.2, s32[]{:T(128)} %constant.154.clone.1..sunk, s32[]{:T(128)S(6)} %select_n.138, s32[]{:T(128)S(6)} %select_n.139) | dynamic-update-slice | bytes 393220 | tf_op jit(solution)/shard_map/while/body/dynamic_update_slice | solution.py:120
  89.7 2.8 %dynamic_update_slice.4 = f32[3,256,256]{2,1,0:T(8,128)S(1)} dynamic-update-slice(f32[3,256,256]{2,1,0:T(8,128)S(1)} %get-tuple-element.257, f32[3,128,128]{2,1,0:T(8,128)S(1)} %maximum_add_fusion.2, s32[]{:T(128)} %constant.154.clone.1..sunk, s32[]{:T(128)S(6)} %select_n.138, s32[]{:T(128)S(6)} %select_n.139) | dynamic-update-slice | bytes 393220 | tf_op jit(solution)/shard_map/while/body/dynamic_update_slice | solution.py:120
  100.5 3.0 %dynamic_update_slice.4 = f32[3,256,256]{2,1,0:T(8,128)S(1)} dynamic-update-slice(f32[3,256,256]{2,1,0:T(8,128)S(1)} %get-tuple-element.257, f32[3,128,128]{2,1,0:T(8,128)S(1)} %maximum_add_fusion.2, s32[]{:T(128)} %constant.154.clone.1..sunk, s32[]{:T(128)S(6)} %select_n.138, s32[]{:T(128)S(6)} %select_n.139) | dynamic-update-slice | bytes 393220 | tf_op jit(solution)/shard_map/while/body/dynamic_update_slice | solution.py:120
  111.5 2.9 %dynamic_update_slice.4 = f32[3,256,256]{2,1,0:T(8,128)S(1)} dynamic-update-slice(f32[3,256,256]{2,1,0:T(8,128)S(1)} %get-tuple-element.257, f32[3,128,128]{2,1,0:T(8,128)S(1)} %maximum_add_fusion.2, s32[]{:T(128)} %constant.154.clone.1..sunk, s32[]{:T(128)S(6)} %select_n.138, s32[]{:T(128)S(6)} %select_n.139) | dynamic-update-slice | bytes 393220 | tf_op jit(solution)/shard_map/while/body/dynamic_update_slice | solution.py:120
  115.1 1.3 collective-permute-start
  116.4 1.0 collective-permute-done
  117.5 1.3 collective-permute-start.1
  118.8 2.0 collective-permute-done.1
  121.0 1.3 collective-permute-start.2
  122.3 1.3 collective-permute-start.3
  123.6 1.8 collective-permute-done.2
  125.6 1.3 scatter-add.16
  126.9 57.1 %collective-permute-done.3 = f32[3,128,64]{2,1,0:T(8,128)S(1)} collective-permute-done((f32[3,128,64]{2,1,0:T(8,128)S(1)}, f32[3,128,64]{2,1,0:T(8,128)S(1)}, u32[]{:S(2)}, u32[]{:S(2)}) %collective-permute-start.3) | collective-permute-done | bytes 98336 | tf_op jit(solution)/shard_map/ppermute | solution.py:33
  184.6 0.8 fusion.145
  185.4 4.8 %collective-permute-start.4 = (bf16[2,64,128]{2,1,0:T(8,128)(2,1)S(1)}, bf16[2,64,128]{2,1,0:T(8,128)(2,1)S(1)}, u32[]{:S(2)}, u32[]{:S(2)}) collective-permute-start(bf16[2,64,128]{2,1,0:T(8,128)(2,1)S(1)} %get-tuple-element.161), channel_id=1, source_target_pairs={{0,8},{8,16},{16,24},{1,9},{9,17},{17,25},{2,10},{10,18},{18,26},{... | collective-permute-start | bytes 98312 | tf_op jit(solution)/shard_map/ppermute | solution.py:44
  190.2 1.3 collective-permute-start.5
  191.5 2.3 collective-permute-done.5
  193.9 1.5 tile.4
  195.4 4.2 %all-to-all-start.2 = ((bf16[2,256,1024]{1,0,2:T(2,128)(2,1)}), bf16[2,256,1024]{1,0,2:T(2,128)(2,1)S(1)}, u32[]{:S(2)}, u32[]{:S(2)}) async-start(bf16[2,256,1024]{1,0,2:T(2,128)(2,1)} %bitcast.15), calls=%async_computation.2 | async-start | bytes 2097152 | tf_op jit(solution)/shard_map/all_to_all | solution.py:15
  199.7 26.4 %all-to-all-done.2 = bf16[2,256,1024]{1,0,2:T(2,128)(2,1)S(1)} async-done(((bf16[2,256,1024]{1,0,2:T(2,128)(2,1)}), bf16[2,256,1024]{1,0,2:T(2,128)(2,1)S(1)}, u32[]{:S(2)}, u32[]{:S(2)}) %all-to-all-start.2) | async-done | bytes 1048608 | tf_op jit(solution)/shard_map/all_to_all | solution.py:15
  226.1 1.5 pad.13
  227.7 9.1 %while.16 = (s32[]{:T(128)}, bf16[2,256,1152]{1,0,2:T(2,128)(2,1)S(1)}, s32[4,3]{1,0:T(4,128)S(1)}, bf16[4,2,128,128]{3,2,0,1:T(8,128)(2,1)S(1)}, s32[]{:T(128)}) while((s32[]{:T(128)}, bf16[2,256,1152]{1,0,2:T(2,128)(2,1)S(1)}, s32[4,3]{1,0:T(4,128)S(1)}, bf16[4,2,128,128]{3,2,0,1:T(8,128)(2,1)S(1)}, s32[]{:T(128)}) %tuple.76), condition=%wide.while_cond.4, body=%wide.while_body.4.sunk | while | flops 2 | bytes 393333 | solution.py:98
  228.3 1.4 constant_dynamic-slice_fusion.9
  230.6 1.4 constant_dynamic-slice_fusion.9
  232.8 1.4 constant_dynamic-slice_fusion.9
  235.1 1.4 constant_dynamic-slice_fusion.9
  236.9 0.8 fusion.18
  238.4 0.8 fusion.7
  242.9 0.8 fusion.34
  243.7 0.8 fusion.38
  244.5 0.8 fusion.5
  246.8 0.8 fusion.4
  (85 shorter events, 23.3 us)
Async XLA Ops:
  4.9 13.8 %all-to-all-start = ((s32[8,2,3]{2,1,0:T(2,128)}), s32[8,2,3]{2,1,0:T(2,128)S(1)}, u32[]{:S(2)}, u32[]{:S(2)}) async-start(s32[8,2,3]{2,1,0:T(2,128)} %bitcast.10), calls=%async_computation | async-start | bytes 16384 | tf_op jit(solution)/shard_map/all_to_all | solution.py:172
  17.7 6.1 %copy-start.1 = (f32[2,128,128]{2,1,0:T(8,128)S(1)}, f32[2,128,128]{2,1,0:T(8,128)}, u32[]{:S(2)}) copy-start(f32[2,128,128]{2,1,0:T(8,128)} %param.17) | copy-start | bytes 393220
  18.7 30.5 %all-to-all-start.1 = ((bf16[16,2,128,128]{3,2,1,0:T(8,128)(2,1)}), bf16[16,2,128,128]{3,2,1,0:T(8,128)(2,1)S(1)}, u32[]{:S(2)}, u32[]{:S(2)}) async-start(bf16[16,2,128,128]{3,2,1,0:T(8,128)(2,1)} %scatter_fusion), calls=%async_computation.1 | async-start | bytes 2097152 | tf_op jit(solution)/shard_map/all_to_all | solution.py:171
  115.1 2.4 collective-permute-start
  117.5 3.3 %collective-permute-start.1 = (f32[3,64,256]{2,1,0:T(8,128)S(1)}, f32[3,64,256]{2,1,0:T(8,128)S(1)}, u32[]{:S(2)}, u32[]{:S(2)}) collective-permute-start(f32[3,64,256]{2,1,0:T(8,128)S(1)} %get-tuple-element.153), channel_id=1, source_target_pairs={{8,0},{16,8},{24,16},{9,1},{17,9},{25,17},{10,2},{18,10},{26,18},{... | collective-permute-start | bytes 589832 | tf_op jit(solution)/shard_map/ppermute | solution.py:33
  121.0 4.5 %collective-permute-start.2 = (f32[3,128,64]{2,1,0:T(8,128)S(1)}, f32[3,128,64]{2,1,0:T(8,128)S(1)}, u32[]{:S(2)}, u32[]{:S(2)}) collective-permute-start(f32[3,128,64]{2,1,0:T(8,128)S(1)} %get-tuple-element.152), channel_id=1, source_target_pairs={{0,1},{1,2},{2,3},{3,4},{4,5},{5,6},{6,7},{8,9},{9,10},{10,11},{11... | collective-permute-start | bytes 294920 | tf_op jit(solution)/shard_map/ppermute | solution.py:33
  122.3 61.7 %collective-permute-start.3 = (f32[3,128,64]{2,1,0:T(8,128)S(1)}, f32[3,128,64]{2,1,0:T(8,128)S(1)}, u32[]{:S(2)}, u32[]{:S(2)}) collective-permute-start(f32[3,128,64]{2,1,0:T(8,128)S(1)} %get-tuple-element.151), channel_id=1, source_target_pairs={{1,0},{2,1},{3,2},{4,3},{5,4},{6,5},{7,6},{9,8},{10,9},{11,10},{12... | collective-permute-start | bytes 294920 | tf_op jit(solution)/shard_map/ppermute | solution.py:33
  185.4 6.1 %collective-permute-start.4 = (bf16[2,64,128]{2,1,0:T(8,128)(2,1)S(1)}, bf16[2,64,128]{2,1,0:T(8,128)(2,1)S(1)}, u32[]{:S(2)}, u32[]{:S(2)}) collective-permute-start(bf16[2,64,128]{2,1,0:T(8,128)(2,1)S(1)} %get-tuple-element.161), channel_id=1, source_target_pairs={{0,8},{8,16},{16,24},{1,9},{9,17},{17,25},{2,10},{10,18},{18,26},{... | collective-permute-start | bytes 98312 | tf_op jit(solution)/shard_map/ppermute | solution.py:44
  190.2 3.6 %collective-permute-start.5 = (bf16[2,64,128]{2,1,0:T(8,128)(2,1)S(1)}, bf16[2,64,128]{2,1,0:T(8,128)(2,1)S(1)}, u32[]{:S(2)}, u32[]{:S(2)}) collective-permute-start(bf16[2,64,128]{2,1,0:T(8,128)(2,1)S(1)} %get-tuple-element.162), channel_id=1, source_target_pairs={{8,0},{16,8},{24,16},{9,1},{17,9},{25,17},{10,2},{18,10},{26,18},{... | collective-permute-start | bytes 98312 | tf_op jit(solution)/shard_map/ppermute | solution.py:46
  195.4 30.7 %all-to-all-start.2 = ((bf16[2,256,1024]{1,0,2:T(2,128)(2,1)}), bf16[2,256,1024]{1,0,2:T(2,128)(2,1)S(1)}, u32[]{:S(2)}, u32[]{:S(2)}) async-start(bf16[2,256,1024]{1,0,2:T(2,128)(2,1)} %bitcast.15), calls=%async_computation.2 | async-start | bytes 2097152 | tf_op jit(solution)/shard_map/all_to_all | solution.py:15
  240.7 2.2 copy-start
